TPU v7x, 32 devices: a whole 2x2x4 slice. The times are simulated.
32 devices in a mesh: depth: 2 (over y), row: 4 (over x, core), col: 4 (over z).
Axes of the slice: x: 2, y: 2, z: 4, core: 2. Of those that a mesh axis runs over, the one named last changes fastest.
Arguments:
- volume: float32 [2, 1024, 1024], P('depth', 'row', 'col'), may hold values from -6 to 6
- psf_spec: float32 [2, 2, 1024, 1024], P(None, 'depth', 'row', 'col'), may hold values from -1.5 to 1.5
- measured: float32 [1024, 1024], P('row', 'col'), may hold values from -6 to 6
- dual: float32 [3, 2, 1024, 1024], P(None, 'depth', 'row', 'col'), may hold values from -3 to 3
Outputs:
- updated: float32 [2, 1024, 1024], P('depth', 'row', 'col')
- shrunk: float32 [3, 2, 1024, 1024], P(None, 'depth', 'row', 'col')
- dual_next: float32 [3, 2, 1024, 1024], P(None, 'depth', 'row', 'col')
All inputs are finite; a program needn't handle non-finite values.
Results may differ from a plain program's by a relative error of at most 0.00005.
Values sent between devices are 32-bit elements; how exact they have to be, the bound alone decides.
A program may use at most 64 MiB of HBM per device.

v0:
```python
import math
import jax
import jax.numpy as jnp
from jax import lax
from jax.sharding import PartitionSpec as P

step_size = 1.0
shrink_level = 0.5
highest = lax.Precision.HIGHEST


def shifted(array, axis, by):
    length = lax.axis_size(axis)
    pairs = [(i, i + by) for i in range(length) if 0 <= i + by < length]
    return lax.ppermute(array, axis, pairs)


def twiddle(first_index, second_index, length, orient):
    phases = first_index[:, None] * second_index[None, :] % length
    angles = phases.astype(jnp.float32) * (orient * 2.0 * math.pi / length)
    return (jnp.cos(angles), jnp.sin(angles))


def complex_mix(field, apply_cos, apply_sin, keep):
    if field.shape[0] == 1:
        real_part = apply_cos(field[0])
        imag_part = apply_sin(field[0])
        return jnp.stack([real_part, imag_part])
    real_part = apply_cos(field[0]) - apply_sin(field[1])
    if keep == 1:
        return real_part[None]
    imag_part = apply_sin(field[0]) + apply_cos(field[1])
    return jnp.stack([real_part, imag_part])


def right_mult(field, cosines, sine_part, keep):

    def apply_cos(part):
        return jnp.dot(part, cosines, precision=highest, preferred_element_type=jnp.float32)

    def apply_sin(part):
        return jnp.dot(part, sine_part, precision=highest, preferred_element_type=jnp.float32)

    return complex_mix(field, apply_cos, apply_sin, keep)


def left_mult(cosines, sine_part, field, keep):

    def apply_cos(part):
        return jnp.einsum(
            "kh,phw->pkw", cosines, part, precision=highest, preferred_element_type=jnp.float32
        )

    def apply_sin(part):
        return jnp.einsum(
            "kh,phw->pkw", sine_part, part, precision=highest, preferred_element_type=jnp.float32
        )

    return complex_mix(field, apply_cos, apply_sin, keep)


def out_parts(field, keep):
    if field.shape[0] == 1:
        return 2
    return keep


def along_columns(field, orient, factor, keep):
    col_block = field.shape[3]
    width_all = col_block * lax.axis_size("col")
    parts_out = out_parts(field, keep)
    targets = lax.axis_index("col") * col_block + jnp.arange(col_block, dtype=jnp.int32)

    def accumulate(running, portion, offset):
        sources = jnp.arange(portion.shape[3], dtype=jnp.int32)
        cosines, sine_part = twiddle(sources, targets, width_all, orient)
        return right_mult(portion, cosines, sine_part, keep)

    start_value = jnp.zeros((parts_out,) + field.shape[1:], jnp.float32)
    result = (
        accumulate(start_value, lax.all_gather(field, "col", axis=3, tiled=True), jnp.int32(0))
        * factor
    )
    return result


def along_rows(field, orient, factor, keep):
    row_block = field.shape[2]
    height_all = row_block * lax.axis_size("row")
    parts_out = out_parts(field, keep)
    targets = lax.axis_index("row") * row_block + jnp.arange(row_block, dtype=jnp.int32)

    def accumulate(running, portion, offset):
        sources = jnp.arange(portion.shape[2], dtype=jnp.int32)
        cosines, sine_part = twiddle(targets, sources, height_all, orient)
        return left_mult(cosines, sine_part, portion, keep)

    start_value = jnp.zeros((parts_out,) + field.shape[1:], jnp.float32)
    result = (
        accumulate(start_value, lax.all_gather(field, "row", axis=2, tiled=True), jnp.int32(0))
        * factor
    )
    return result


def shards(volume, psf_spec, measured, dual):
    planes, row_block, col_block = volume.shape
    height_all = row_block * lax.axis_size("row")
    width_all = col_block * lax.axis_size("col")
    spectra = along_rows(along_columns(volume[None], -1.0, 1.0, 2), -1.0, 1.0, 2)
    kernel_real = psf_spec[0]
    kernel_imag = psf_spec[1]
    prod_real = jnp.sum(kernel_real * spectra[0] - kernel_imag * spectra[1], axis=0, keepdims=True)
    prod_imag = jnp.sum(kernel_real * spectra[1] + kernel_imag * spectra[0], axis=0, keepdims=True)
    local_sum = jnp.stack([prod_real, prod_imag])
    row_global = lax.axis_index("row") * row_block + jnp.arange(row_block, dtype=jnp.int32)
    col_global = lax.axis_index("col") * col_block + jnp.arange(col_block, dtype=jnp.int32)
    inside = ((row_global >= height_all // 4) & (row_global < 3 * height_all // 4))[:, None] & (
        (col_global >= width_all // 4) & (col_global < 3 * width_all // 4)
    )[None, :]
    empty_part = jnp.zeros_like(measured)
    summed_image = lax.psum(local_sum, "depth")
    sensor_image = along_columns(
        along_rows(summed_image, 1.0, 1.0 / height_all, 2), 1.0, 1.0 / width_all, 1
    )[0, 0]
    residual_map = jnp.where(inside, sensor_image - measured, empty_part)
    residual_spec = along_rows(along_columns(residual_map[None, None], -1.0, 1.0, 2), -1.0, 1.0, 2)
    back_real = kernel_real * residual_spec[0] + kernel_imag * residual_spec[1]
    back_imag = kernel_real * residual_spec[1] - kernel_imag * residual_spec[0]
    adjoint = along_columns(
        along_rows(jnp.stack([back_real, back_imag]), 1.0, 1.0 / height_all, 2),
        1.0,
        1.0 / width_all,
        1,
    )[0]
    updated = volume - step_size * adjoint
    plane_ahead = shifted(updated, "depth", -1)
    depth_count = planes * lax.axis_size("depth")
    plane_global = lax.axis_index("depth") * planes + jnp.arange(planes, dtype=jnp.int32)
    diff_depth = jnp.where(
        (plane_global < depth_count - 1)[:, None, None],
        jnp.concatenate([updated[1:], plane_ahead], axis=0) - updated,
        0.0,
    )
    row_ahead = shifted(updated[:, :1, :], "row", -1)
    diff_rows = jnp.where(
        (row_global < height_all - 1)[None, :, None],
        jnp.concatenate([updated[:, 1:, :], row_ahead], axis=1) - updated,
        0.0,
    )
    col_ahead = shifted(updated[:, :, :1], "col", -1)
    diff_cols = jnp.where(
        (col_global < width_all - 1)[None, None, :],
        jnp.concatenate([updated[:, :, 1:], col_ahead], axis=2) - updated,
        0.0,
    )
    combined = jnp.stack([diff_depth, diff_rows, diff_cols]) + dual
    dual_next = jnp.clip(combined, -shrink_level, shrink_level)
    return (updated, combined - dual_next, dual_next)


def solution(mesh):
    placed = (
        P("depth", "row", "col"),
        P(None, "depth", "row", "col"),
        P("row", "col"),
        P(None, "depth", "row", "col"),
    )
    return jax.shard_map(
        shards,
        mesh=mesh,
        in_specs=placed,
        out_specs=(
            P("depth", "row", "col"),
            P(None, "depth", "row", "col"),
            P(None, "depth", "row", "col"),
        ),
        check_vma=False,
    )
```

profile of v0, /device:TPU:0, one launch (start us, length us, event | category | flops | bytes accessed | tf_op | source)
XLA Modules:
  0.0 439.6 jit_solution(15999376654098091278)
XLA Ops:
  7.2 0.7 all-gather.23.cloned.1.call-update
  8.0 32.3 %all-gather.23.cloned.1.call-done = f32[1,256,1024]{2,1,0:T(8,128)} async-done(((f32[1,256,256]{2,1,0:T(8,128)}), f32[1,256,1024]{2,1,0:T(8,128)}) %all-gather.23.cloned.1.call-update) | async-done | bytes 1048592 | tf_op jit(solution)/shard_map/all_gather | solution.py:81
  40.3 6.9 %convolution_bitcast_fusion.2 = f32[1,1,256,256]{2,3,1,0:T(8,128)S(1)} fusion(f32[1,256,1024]{2,1,0:T(8,128)} %all-gather.23.cloned.1.call-done, s32[256]{0:T(256)S(1)} %iota_add_fusion), kind=kOutput, calls=%fused_computation.31 | convolution fusion | flops 808976384 | bytes 1311744 | tf_op jit(solution)/shard_map/dot_general | solution.py:42
  47.2 5.6 %convolution_bitcast_fusion.3 = f32[1,1,256,256]{2,3,1,0:T(8,128)S(1)} fusion(f32[1,256,1024]{2,1,0:T(8,128)S(1)} %copy-done.10, s32[256]{0:T(256)S(1)} %iota_add_fusion), kind=kOutput, calls=%fused_computation.32 | convolution fusion | flops 808976384 | bytes 1311744 | tf_op jit(solution)/shard_map/dot_general | solution.py:39
  52.8 0.8 pad_maximum_fusion
  53.6 0.3 all-reduce.2.cloned.1.call-start
  54.2 21.5 %all-gather.11.cloned.1.call-done = f32[2,1,1024,256]{2,3,1,0:T(8,128)} async-done(((f32[2,1,256,256]{2,3,1,0:T(8,128)}), f32[2,1,1024,256]{2,3,1,0:T(8,128)}) %all-gather.11.cloned.1.call-update) | async-done | bytes 2097168 | tf_op jit(solution)/shard_map/all_gather | solution.py:100
  75.7 6.3 %fusion.28 = f32[256,256]{1,0:T(8,128)S(1)} fusion(f32[2,1,1024,256]{2,3,1,0:T(8,128)} %all-gather.11.cloned.1.call-done, s32[256]{0:T(256)S(1)} %iota_add_fusion.1), kind=kOutput, calls=%fused_computation.60 | convolution fusion | flops 808976384 | bytes 1311744 | tf_op jit(solution)/shard_map/kh,phw->pkw/dot_general | solution.py:55
  82.0 4.9 %fusion.29 = f32[256,256]{1,0:T(8,128)S(1)} fusion(f32[2,1,1024,256]{2,3,1,0:T(8,128)S(1)} %copy-done.4, s32[256]{0:T(256)S(1)} %iota_add_fusion.1), kind=kOutput, calls=%fused_computation.61 | convolution fusion | flops 808976384 | bytes 1311744 | tf_op jit(solution)/shard_map/kh,phw->pkw/dot_general | solution.py:50
  86.9 5.3 %fusion.11 = f32[1,256,256]{1,2,0:T(8,128)S(1)} fusion(f32[256,256]{1,0:T(8,128)S(1)} %fusion.28, f32[2,1,1024,256]{2,3,1,0:T(8,128)S(1)} %copy-done.4, s32[256]{0:T(256)S(1)} %iota_add_fusion.1), kind=kOutput, calls=%fused_computation.28 | convolution fusion | flops 809041920 | bytes 1573888 | tf_op jit(solution)/shard_map/kh,phw->pkw/dot_general | solution.py:50
  92.2 4.9 %fusion.89 = (f32[1,1,256,256]{2,3,1,0:T(8,128)S(1)}, f32[1,1,256,256]{2,3,1,0:T(8,128)S(1)}) fusion(f32[1,256,256]{1,2,0:T(8,128)S(1)} %fusion.11, f32[1,1,256,256]{2,3,1,0:T(8,128)S(1)} %copy.10, f32[1,1,256,256]{2,3,1,0:T(8,128)S(1)} %copy.9, f32[256,256]{1,0:T(8,128)S(1)} %fusion.29, s32[256]{0:T(256)S(1)} %iota_add_fusion.1, ...), kind=kOutput, calls=%fused_computation.119 | convolution fusion | flops 809435136 | bytes 2622464 | tf_op jit(solution)/shard_map/kh,phw->pkw/dot_general | solution.py:55
  97.2 0.8 pad_maximum_fusion.1
  98.1 28.8 %all-reduce.2.cloned.1.call-done = f32[2,1,256,256]{2,3,1,0:T(8,128)} async-done(((f32[2,1,256,256]{2,3,1,0:T(8,128)}), f32[2,1,256,256]{2,3,1,0:T(8,128)}) %all-reduce.2.cloned.1.call-update) | async-done | bytes 524304 | tf_op jit(solution)/shard_map/psum | solution.py:122
  127.1 23.8 %all-gather.13.cloned.1.call-done = f32[2,1,1024,256]{2,3,1,0:T(8,128)} async-done(((f32[2,1,256,256]{2,3,1,0:T(8,128)}), f32[2,1,1024,256]{2,3,1,0:T(8,128)}) %all-gather.13.cloned.1.call-update) | async-done | bytes 2097168 | tf_op jit(solution)/shard_map/all_gather | solution.py:100
  150.9 6.3 %fusion.30 = f32[256,256]{1,0:T(8,128)S(1)} fusion(f32[2,1,1024,256]{2,3,1,0:T(8,128)} %all-gather.13.cloned.1.call-done, s32[256]{0:T(256)S(1)} %iota_add_fusion.1), kind=kOutput, calls=%fused_computation.62 | convolution fusion | flops 808976384 | bytes 1311744 | tf_op jit(solution)/shard_map/kh,phw->pkw/dot_general | solution.py:55
  157.2 4.9 %fusion.31 = f32[256,256]{1,0:T(8,128)S(1)} fusion(f32[2,1,1024,256]{2,3,1,0:T(8,128)S(1)} %copy-done.8, s32[256]{0:T(256)S(1)} %iota_add_fusion.1), kind=kOutput, calls=%fused_computation.63 | convolution fusion | flops 808976384 | bytes 1311744 | tf_op jit(solution)/shard_map/kh,phw->pkw/dot_general | solution.py:50
  162.1 5.1 %fusion.9 = f32[1,1,256,256]{2,3,1,0:T(8,128)S(1)} fusion(f32[256,256]{1,0:T(8,128)S(1)} %fusion.30, f32[2,1,1024,256]{2,3,1,0:T(8,128)S(1)} %copy-done.8, s32[256]{0:T(256)S(1)} %iota_add_fusion.1), kind=kOutput, calls=%fused_computation.24 | convolution fusion | flops 809041920 | bytes 1573888 | tf_op jit(solution)/shard_map/kh,phw->pkw/dot_general | solution.py:50
  167.2 4.9 %fusion.10 = f32[1,1,256,256]{2,3,1,0:T(8,128)S(1)} fusion(f32[256,256]{1,0:T(8,128)S(1)} %fusion.31, f32[2,1,1024,256]{2,3,1,0:T(8,128)S(1)} %copy-done.8, s32[256]{0:T(256)S(1)} %iota_add_fusion.1), kind=kOutput, calls=%fused_computation.26 | convolution fusion | flops 809041920 | bytes 1573888 | tf_op jit(solution)/shard_map/kh,phw->pkw/dot_general | solution.py:55
  172.1 0.8 maximum_multiply_fusion
  173.0 0.4 all-gather.25.cloned.1.call-start
  173.5 45.3 %all-gather.15.cloned.1.call-done = f32[2,1,256,1024]{2,3,1,0:T(8,128)} async-done(((f32[2,1,256,256]{2,3,1,0:T(8,128)}), f32[2,1,256,1024]{2,3,1,0:T(8,128)}) %all-gather.15.cloned.1.call-update) | async-done | bytes 2097168 | tf_op jit(solution)/shard_map/all_gather | solution.py:81
  218.8 6.9 %fusion.19 = f32[256,256]{1,0:T(8,128)S(1)} fusion(f32[2,1,256,1024]{2,3,1,0:T(8,128)} %all-gather.15.cloned.1.call-done, s32[256]{0:T(256)S(1)} %iota_add_fusion), kind=kOutput, calls=%fused_computation.47 | convolution fusion | flops 808976384 | bytes 1311744 | tf_op jit(solution)/shard_map/dot_general | solution.py:39
  225.7 6.3 %fusion.8 = f32[256,256]{1,0:T(8,128)} fusion(f32[256,256]{1,0:T(8,128)S(1)} %copy-done.12, f32[256,256]{1,0:T(8,128)S(1)} %fusion.19, f32[2,1,256,1024]{2,3,1,0:T(8,128)S(1)} %copy-done.6, s32[256]{0:T(256)S(1)} %iota_add_fusion, pred[256]{0:T(512)(128)(4,1)S(1)} %get-tuple-element.14, pred[256]{0:T(512)(128)(4,1)S(1)} %get-tuple-element.15), kind=kOutput, calls=%fused_computation.22 | convolution fusion | flops 809304064 | bytes 1837056 | tf_op jit(solution)/shard_map/dot_general | solution.py:42
  232.2 26.7 %all-gather.25.cloned.1.call-done = f32[256,1024]{1,0:T(8,128)} async-done(((f32[256,256]{1,0:T(8,128)}), f32[256,1024]{1,0:T(8,128)}) %all-gather.25.cloned.1.call-update) | async-done | bytes 1048592 | tf_op jit(solution)/shard_map/all_gather | solution.py:81
  258.9 6.2 %convolution_bitcast_fusion = f32[1,1,256,256]{3,2,1,0:T(8,128)S(1)} fusion(f32[256,1024]{1,0:T(8,128)} %all-gather.25.cloned.1.call-done, s32[256]{0:T(256)S(1)} %iota_add_fusion), kind=kOutput, calls=%fused_computation.17 | convolution fusion | flops 808976384 | bytes 1311744 | tf_op jit(solution)/shard_map/dot_general | solution.py:42
  265.1 4.8 %convolution_bitcast_fusion.1 = f32[1,1,256,256]{3,2,1,0:T(8,128)S(1)} fusion(f32[256,1024]{1,0:T(8,128)S(1)} %copy-done.11, s32[256]{0:T(256)S(1)} %iota_add_fusion), kind=kOutput, calls=%fused_computation.18 | convolution fusion | flops 808976384 | bytes 1311744 | tf_op jit(solution)/shard_map/dot_general | solution.py:39
  270.0 0.8 pad_maximum_fusion.2
  271.1 21.8 %all-gather.17.cloned.1.call-done = f32[2,1,1024,256]{3,2,1,0:T(8,128)} async-done(((f32[2,1,256,256]{3,2,1,0:T(8,128)}), f32[2,1,1024,256]{3,2,1,0:T(8,128)}) %all-gather.17.cloned.1.call-update) | async-done | bytes 2097168 | tf_op jit(solution)/shard_map/all_gather | solution.py:100
  292.9 6.9 %fusion.32 = f32[256,256]{1,0:T(8,128)S(1)} fusion(f32[2,1,1024,256]{3,2,1,0:T(8,128)} %all-gather.17.cloned.1.call-done, s32[256]{0:T(256)S(1)} %iota_add_fusion.1), kind=kOutput, calls=%fused_computation.64 | convolution fusion | flops 808976384 | bytes 1311744 | tf_op jit(solution)/shard_map/kh,phw->pkw/dot_general | solution.py:55
  299.9 5.6 %fusion.33 = f32[256,256]{1,0:T(8,128)S(1)} fusion(f32[2,1,1024,256]{3,2,1,0:T(8,128)S(1)} %copy-done.5, s32[256]{0:T(256)S(1)} %iota_add_fusion.1), kind=kOutput, calls=%fused_computation.65 | convolution fusion | flops 808976384 | bytes 1311744 | tf_op jit(solution)/shard_map/kh,phw->pkw/dot_general | solution.py:50
  305.4 6.0 %fusion.4 = f32[1,256,256]{1,2,0:T(8,128)S(1)} fusion(f32[256,256]{1,0:T(8,128)S(1)} %fusion.32, f32[2,1,1024,256]{3,2,1,0:T(8,128)S(1)} %copy-done.5, s32[256]{0:T(256)S(1)} %iota_add_fusion.1), kind=kOutput, calls=%fused_computation.14 | convolution fusion | flops 809041920 | bytes 1573888 | tf_op jit(solution)/shard_map/kh,phw->pkw/dot_general | solution.py:50
  311.4 5.6 %fusion.93 = (f32[1,1,256,256]{2,3,1,0:T(8,128)S(1)}, f32[1,1,256,256]{2,3,1,0:T(8,128)S(1)}) fusion(f32[1,256,256]{1,2,0:T(8,128)S(1)} %fusion.4, f32[1,1,256,256]{2,3,1,0:T(8,128)S(1)} %copy.10, f32[1,1,256,256]{2,3,1,0:T(8,128)S(1)} %copy.9, f32[256,256]{1,0:T(8,128)S(1)} %fusion.33, s32[256]{0:T(256)S(1)} %iota_add_fusion.1, ...), kind=kOutput, calls=%fused_computation.123 | convolution fusion | flops 809435136 | bytes 2622464 | tf_op jit(solution)/shard_map/kh,phw->pkw/dot_general | solution.py:55
  317.0 0.8 pad_maximum_fusion.3
  318.1 22.5 %all-gather.19.cloned.1.call-done = f32[2,1,1024,256]{2,3,1,0:T(8,128)} async-done(((f32[2,1,256,256]{2,3,1,0:T(8,128)}), f32[2,1,1024,256]{2,3,1,0:T(8,128)}) %all-gather.19.cloned.1.call-update) | async-done | bytes 2097168 | tf_op jit(solution)/shard_map/all_gather | solution.py:100
  340.6 6.3 %fusion.34 = f32[256,256]{1,0:T(8,128)S(1)} fusion(f32[2,1,1024,256]{2,3,1,0:T(8,128)} %all-gather.19.cloned.1.call-done, s32[256]{0:T(256)S(1)} %iota_add_fusion.1), kind=kOutput, calls=%fused_computation.66 | convolution fusion | flops 808976384 | bytes 1311744 | tf_op jit(solution)/shard_map/kh,phw->pkw/dot_general | solution.py:55
  346.9 4.9 %fusion.35 = f32[256,256]{1,0:T(8,128)S(1)} fusion(f32[2,1,1024,256]{2,3,1,0:T(8,128)S(1)} %copy-done.7, s32[256]{0:T(256)S(1)} %iota_add_fusion.1), kind=kOutput, calls=%fused_computation.67 | convolution fusion | flops 808976384 | bytes 1311744 | tf_op jit(solution)/shard_map/kh,phw->pkw/dot_general | solution.py:50
  351.8 5.1 %fusion.2 = f32[1,1,256,256]{2,3,1,0:T(8,128)S(1)} fusion(f32[256,256]{1,0:T(8,128)S(1)} %fusion.34, f32[2,1,1024,256]{2,3,1,0:T(8,128)S(1)} %copy-done.7, s32[256]{0:T(256)S(1)} %iota_add_fusion.1), kind=kOutput, calls=%fused_computation.10 | convolution fusion | flops 809041920 | bytes 1573888 | tf_op jit(solution)/shard_map/kh,phw->pkw/dot_general | solution.py:50
  356.9 4.9 %fusion.3 = f32[1,1,256,256]{2,3,1,0:T(8,128)S(1)} fusion(f32[256,256]{1,0:T(8,128)S(1)} %fusion.35, f32[2,1,1024,256]{2,3,1,0:T(8,128)S(1)} %copy-done.7, s32[256]{0:T(256)S(1)} %iota_add_fusion.1), kind=kOutput, calls=%fused_computation.12 | convolution fusion | flops 809041920 | bytes 1573888 | tf_op jit(solution)/shard_map/kh,phw->pkw/dot_general | solution.py:55
  361.8 0.8 maximum_multiply_fusion.1
  362.7 45.8 %all-gather.21.cloned.1.call-done = f32[2,1,256,1024]{2,3,1,0:T(8,128)} async-done(((f32[2,1,256,256]{2,3,1,0:T(8,128)}), f32[2,1,256,1024]{2,3,1,0:T(8,128)}) %all-gather.21.cloned.1.call-update) | async-done | bytes 2097168 | tf_op jit(solution)/shard_map/all_gather | solution.py:81
  408.5 7.1 %fusion.18 = f32[256,256]{1,0:T(8,128)S(1)} fusion(f32[2,1,256,1024]{2,3,1,0:T(8,128)} %all-gather.21.cloned.1.call-done, s32[256]{0:T(256)S(1)} %iota_add_fusion), kind=kOutput, calls=%fused_computation.40 | convolution fusion | flops 808976384 | bytes 1311744 | tf_op jit(solution)/shard_map/dot_general | solution.py:39
  415.7 5.5 %fusion.13 = f32[1,256,256]{2,1,0:T(8,128)S(1)} fusion(f32[1,256,256]{2,1,0:T(8,128)S(1)} %copy-done.3, f32[256,256]{1,0:T(8,128)S(1)} %fusion.18, f32[2,1,256,1024]{2,3,1,0:T(8,128)S(1)} %copy-done.9, s32[256]{0:T(256)S(1)} %iota_add_fusion), kind=kOutput, calls=%fused_computation.33 | convolution fusion | flops 809172992 | bytes 1836032 | tf_op jit(solution)/shard_map/dot_general | solution.py:42
  421.2 1.4 collective-permute-start
  422.7 1.3 collective-permute-start.2
  424.0 1.3 collective-permute-start.1
  425.5 4.2 collective-permute-done.2
  429.7 1.5 collective-permute-done
  431.3 1.3 fusion.96
  (54 shorter events, 1.8 us)
Async XLA Ops:
  7.2 33.1 %all-gather.23.cloned.1.call-start = ((), (), s32[]{:S(2)}) async-start(), calls=%async_computation.7 | async-start | bytes 1310720 | tf_op jit(solution)/shard_map/all_gather | solution.py:81
  7.9 67.8 %all-gather.11.cloned.1.call-start = ((), (), s32[]{:S(2)}) async-start(), calls=%async_computation | async-start | bytes 2621440 | tf_op jit(solution)/shard_map/all_gather | solution.py:100
  40.3 6.9 %copy-start.10 = (f32[1,256,1024]{2,1,0:T(8,128)S(1)}, f32[1,256,1024]{2,1,0:T(8,128)}, u32[]{:S(2)}) copy-start(f32[1,256,1024]{2,1,0:T(8,128)} %all-gather.23.cloned.1.call-done) | copy-start | bytes 3145732
  47.2 6.7 %copy-start.2 = (f32[2,1,256,256]{3,2,1,0:T(8,128)S(1)}, f32[2,1,256,256]{3,2,1,0:T(8,128)}, u32[]{:S(2)}) copy-start(f32[2,1,256,256]{3,2,1,0:T(8,128)} %param.5) | copy-start | bytes 1572868
  53.6 73.2 %all-reduce.2.cloned.1.call-start = ((), (), s32[]{:S(2)}) async-start(), calls=%async_computation.1 | async-start | bytes 1048576 | tf_op jit(solution)/shard_map/psum | solution.py:122
  75.7 6.3 %copy-start.4 = (f32[2,1,1024,256]{2,3,1,0:T(8,128)S(1)}, f32[2,1,1024,256]{2,3,1,0:T(8,128)}, u32[]{:S(2)}) copy-start(f32[2,1,1024,256]{2,3,1,0:T(8,128)} %all-gather.11.cloned.1.call-done) | copy-start | bytes 6291460
  98.0 52.8 %all-gather.13.cloned.1.call-start = ((), (), s32[]{:S(2)}) async-start(), calls=%async_computation.2 | async-start | bytes 2621440 | tf_op jit(solution)/shard_map/all_gather | solution.py:100
  126.9 91.9 %all-gather.15.cloned.1.call-start = ((), (), s32[]{:S(2)}) async-start(), calls=%async_computation.3 | async-start | bytes 2621440 | tf_op jit(solution)/shard_map/all_gather | solution.py:81
  150.9 6.3 %copy-start.8 = (f32[2,1,1024,256]{2,3,1,0:T(8,128)S(1)}, f32[2,1,1024,256]{2,3,1,0:T(8,128)}, u32[]{:S(2)}) copy-start(f32[2,1,1024,256]{2,3,1,0:T(8,128)} %all-gather.13.cloned.1.call-done) | copy-start | bytes 6291460
  173.0 85.9 %all-gather.25.cloned.1.call-start = ((), (), s32[]{:S(2)}) async-start(), calls=%async_computation.8 | async-start | bytes 1310720 | tf_op jit(solution)/shard_map/all_gather | solution.py:81
  173.4 52.2 %copy-start.12 = (f32[256,256]{1,0:T(8,128)S(1)}, f32[256,256]{1,0:T(8,128)}, u32[]{:S(2)}) copy-start(f32[256,256]{1,0:T(8,128)} %param.6) | copy-start | bytes 786436
  218.8 6.9 %copy-start.6 = (f32[2,1,256,1024]{2,3,1,0:T(8,128)S(1)}, f32[2,1,256,1024]{2,3,1,0:T(8,128)}, u32[]{:S(2)}) copy-start(f32[2,1,256,1024]{2,3,1,0:T(8,128)} %all-gather.15.cloned.1.call-done) | copy-start | bytes 6291460
  232.0 60.9 %all-gather.17.cloned.1.call-start = ((), (), s32[]{:S(2)}) async-start(), calls=%async_computation.4 | async-start | bytes 2621440 | tf_op jit(solution)/shard_map/all_gather | solution.py:100
  258.9 6.2 %copy-start.11 = (f32[256,1024]{1,0:T(8,128)S(1)}, f32[256,1024]{1,0:T(8,128)}, u32[]{:S(2)}) copy-start(f32[256,1024]{1,0:T(8,128)} %all-gather.25.cloned.1.call-done) | copy-start | bytes 3145732
  270.8 69.7 %all-gather.19.cloned.1.call-start = ((), (), s32[]{:S(2)}) async-start(), calls=%async_computation.5 | async-start | bytes 2621440 | tf_op jit(solution)/shard_map/all_gather | solution.py:100
  292.9 7.0 %copy-start.5 = (f32[2,1,1024,256]{3,2,1,0:T(8,128)S(1)}, f32[2,1,1024,256]{3,2,1,0:T(8,128)}, u32[]{:S(2)}) copy-start(f32[2,1,1024,256]{3,2,1,0:T(8,128)} %all-gather.17.cloned.1.call-done) | copy-start | bytes 6291460
  317.9 90.6 %all-gather.21.cloned.1.call-start = ((), (), s32[]{:S(2)}) async-start(), calls=%async_computation.6 | async-start | bytes 2621440 | tf_op jit(solution)/shard_map/all_gather | solution.py:81
  340.6 6.3 %copy-start.7 = (f32[2,1,1024,256]{2,3,1,0:T(8,128)S(1)}, f32[2,1,1024,256]{2,3,1,0:T(8,128)}, u32[]{:S(2)}) copy-start(f32[2,1,1024,256]{2,3,1,0:T(8,128)} %all-gather.19.cloned.1.call-done) | copy-start | bytes 6291460
  362.7 53.0 %copy-start.3 = (f32[1,256,256]{2,1,0:T(8,128)S(1)}, f32[1,256,256]{2,1,0:T(8,128)}, u32[]{:S(2)}) copy-start(f32[1,256,256]{2,1,0:T(8,128)} %param.4) | copy-start | bytes 786436
  408.5 7.1 %copy-start.9 = (f32[2,1,256,1024]{2,3,1,0:T(8,128)S(1)}, f32[2,1,256,1024]{2,3,1,0:T(8,128)}, u32[]{:S(2)}) copy-start(f32[2,1,256,1024]{2,3,1,0:T(8,128)} %all-gather.21.cloned.1.call-done) | copy-start | bytes 6291460
  421.2 11.4 %copy-start = (f32[1,256,256]{2,1,0:T(8,128)}, f32[1,256,256]{2,1,0:T(8,128)S(1)}, u32[]{:S(2)}) copy-start(f32[1,256,256]{2,1,0:T(8,128)S(1)} %fusion.13) | copy-start | bytes 786436
  421.2 10.1 %copy-start.1 = (f32[3,1,256,256]{3,2,1,0:T(8,128)S(1)}, f32[3,1,256,256]{3,2,1,0:T(8,128)}, u32[]{:S(2)}) copy-start(f32[3,1,256,256]{3,2,1,0:T(8,128)} %param.7) | copy-start | bytes 2359300
  421.2 9.9 %collective-permute-start = (f32[1,256,256]{2,1,0:T(8,128)S(1)}, f32[1,256,256]{2,1,0:T(8,128)S(1)}, u32[]{:S(2)}, u32[]{:S(2)}) collective-permute-start(f32[1,256,256]{2,1,0:T(8,128)S(1)} %fusion.13), channel_id=1, source_target_pairs={{16,0},{17,1},{18,2},{19,3},{20,4},{21,5},{22,6},{23,7},{24,8},{25... | collective-permute-start | bytes 786440 | tf_op jit(solution)/shard_map/ppermute | solution.py:15
  422.7 7.0 %collective-permute-start.2 = (f32[1,256,1]{2,1,0:T(8,128)S(1)}, f32[1,256,1]{2,1,0:T(8,128)S(1)}, u32[]{:S(2)}, u32[]{:S(2)}) collective-permute-start(f32[1,256,1]{2,1,0:T(8,128)S(1)} %slice.95), channel_id=1, source_target_pairs={{1,0},{2,1},{3,2},{5,4},{6,5},{7,6},{9,8},{10,9},{11,10},{13,12},{... | collective-permute-start | bytes 3080 | tf_op jit(solution)/shard_map/ppermute | solution.py:15
  424.0 5.7 %collective-permute-start.1 = (f32[1,1,256]{2,1,0:T(1,128)S(1)}, f32[1,1,256]{2,1,0:T(1,128)S(1)}, u32[]{:S(2)}, u32[]{:S(2)}) collective-permute-start(f32[1,1,256]{2,1,0:T(1,128)S(1)} %slice.93), channel_id=1, source_target_pairs={{4,0},{8,4},{12,8},{5,1},{9,5},{13,9},{6,2},{10,6},{14,10},{7,3},{... | collective-permute-start | bytes 3080 | tf_op jit(solution)/shard_map/ppermute | solution.py:15
Sparse Core Ops, SparseCore 0:
  9.5 30.6 all-gather.22
  53.8 21.9 all-gather.10
  98.2 28.6 all-reduce.1
  128.3 22.5 all-gather.12
  173.1 45.6 all-gather.14
  232.1 26.7 all-gather.24
  270.9 21.9 all-gather.16
  318.0 22.5 all-gather.18
  362.8 45.6 all-gather.20
where the time goes:
time: 448 us; the launch traced here: 440 us
  waiting for transfers between devices  275 us (61%)
  matrix products  137 us (31%)
  between operations  14.7 us (3%)
  other arithmetic  6.46 us (1%)
  starting transfers between devices  5.72 us (1%)
    all_gather x4, waiting for transfers between devices, along_columns(): lax.all_gather(field, 'col', axis=3, tiled=True)  150 us
    all_gather x4, waiting for transfers between devices, along_rows(): lax.all_gather(field, 'row', axis=2, tiled=True)  89.6 us
    dot_general x8, matrix products, apply_sin(): jnp.einsum('kh,phw->pkw', sine_part, part, precision=highest, preferred_e...  46.2 us
    dot_general x8, matrix products, apply_cos(): jnp.einsum('kh,phw->pkw', cosines, part, precision=highest, preferred_ele...  41.7 us
    psum x1, waiting for transfers between devices, shards(): summed_image = lax.psum(local_sum, 'depth')  28.8 us
    dot_general x4, matrix products, apply_sin(): jnp.dot(part, sine_part, precision=highest, preferred_element_type=jnp.fl...  24.9 us
    dot_general x4, matrix products, apply_cos(): jnp.dot(part, cosines, precision=highest, preferred_element_type=jnp.floa...  24.4 us
  transfers between devices with their start and end apart: 12, of which 11 were waited for; matrix products, arithmetic and copies ran while one was open for 0% of the time, Pallas kernels for 0%

commit v1 on v0

--- a/solution.py
+++ b/solution.py
@@ -7,6 +7,14 @@
 step_size = 1.0
 shrink_level = 0.5
 highest = lax.Precision.HIGHEST
+
+
+def tiled_gather(array, axis, dim):
+    count = lax.axis_size(axis)
+    repeats = [count if d == dim else 1 for d in range(array.ndim)]
+    return lax.all_to_all(
+        jnp.tile(array, repeats), axis, split_axis=dim, concat_axis=dim, tiled=True
+    )
 
 
 def shifted(array, axis, by):
@@ -96,10 +104,7 @@
         return left_mult(cosines, sine_part, portion, keep)
 
     start_value = jnp.zeros((parts_out,) + field.shape[1:], jnp.float32)
-    result = (
-        accumulate(start_value, lax.all_gather(field, "row", axis=2, tiled=True), jnp.int32(0))
-        * factor
-    )
+    result = accumulate(start_value, tiled_gather(field, "row", 2), jnp.int32(0)) * factor
     return result
 
 

time: 448 us -> 481 us (1.074)
  blocking collectives: 0 us -> 84.5 us
  waiting for transfers between devices: 275 us -> 207 us
  local copies, waits for them, and re-layouts: 0.51 us -> 12.8 us
    all_gather x4 -> x0, waiting for transfers between devices: 89.6 us -> none  [along_rows(): lax.all_gather(field, 'row', axis=2, tiled=True)]
    all_to_all x0 -> x3, blocking collectives: none -> 84.5 us  [tiled_gather(): lax.all_to_all(jnp.tile(array, repeats), axis, split_axis=dim, concat_axi...]
    all_to_all x0 -> x1, waiting for transfers between devices: none -> 25.2 us  [tiled_gather(): lax.all_to_all(jnp.tile(array, repeats), axis, split_axis=dim, concat_axi...]
    slice x0 -> x4, local copies, waits for them, and re-layouts: none -> 6.47 us  [complex_mix(): real_part = apply_cos(field[0]) - apply_sin(field[1])]
  transfers between devices with their start and end apart: 12 -> 9, of which waited for: 11 -> 8; matrix products, arithmetic and copies ran while one was open for 0% -> 0% of each run, Pallas kernels for 0% -> 0%
where the time goes in v1:
time: 481 us; the launch traced here: 472 us
  waiting for transfers between devices  207 us (43%)
  matrix products  141 us (29%)
  blocking collectives  84.5 us (18%)
  between operations  14.7 us (3%)
  local copies, waits for them, and re-layouts  12.8 us (3%)
  starting transfers between devices  8.16 us (2%)
    all_gather x4, waiting for transfers between devices, along_columns(): lax.all_gather(field, 'col', axis=3, tiled=True)  148 us
    all_to_all x3, blocking collectives, tiled_gather(): lax.all_to_all(jnp.tile(array, repeats), axis, split_axis=dim, concat_axi...  84.5 us
    dot_general x8, matrix products, apply_sin(): jnp.einsum('kh,phw->pkw', sine_part, part, precision=highest, preferred_e...  46.3 us
    dot_general x8, matrix products, apply_cos(): jnp.einsum('kh,phw->pkw', cosines, part, precision=highest, preferred_ele...  45.8 us
    psum x1, waiting for transfers between devices, shards(): summed_image = lax.psum(local_sum, 'depth')  27.2 us
    dot_general x4, matrix products, apply_cos(): jnp.dot(part, cosines, precision=highest, preferred_element_type=jnp.floa...  25.5 us
    all_to_all x1, waiting for transfers between devices, tiled_gather(): lax.all_to_all(jnp.tile(array, repeats), axis, split_axis=dim, concat_axi...  25.2 us
    dot_general x4, matrix products, apply_sin(): jnp.dot(part, sine_part, precision=highest, preferred_element_type=jnp.fl...  23.6 us
  transfers between devices with their start and end apart: 9, of which 8 were waited for; matrix products, arithmetic and copies ran while one was open for 0% of the time, Pallas kernels for 0%

profile of v1, /device:TPU:0, one launch (start us, length us, event | category | flops | bytes accessed | tf_op | source)
XLA Modules:
  0.0 472.4 jit_solution(15797672033838252894)
XLA Ops:
  7.9 32.4 %all-gather.11.cloned.1.call-done = f32[1,256,1024]{2,1,0:T(8,128)} async-done(((f32[1,256,256]{2,1,0:T(8,128)}), f32[1,256,1024]{2,1,0:T(8,128)}) %all-gather.11.cloned.1.call-update) | async-done | bytes 1048592 | tf_op jit(solution)/shard_map/all_gather | solution.py:89
  40.3 6.9 %convolution_bitcast_fusion.2 = f32[1,1,256,256]{2,3,1,0:T(8,128)S(1)} fusion(f32[1,256,1024]{2,1,0:T(8,128)} %all-gather.11.cloned.1.call-done, s32[256]{0:T(256)S(1)} %iota_add_fusion), kind=kOutput, calls=%fused_computation.31 | convolution fusion | flops 808976384 | bytes 1311744 | tf_op jit(solution)/shard_map/dot_general | solution.py:50
  47.2 5.6 %convolution_bitcast_fusion.3 = f32[1,1,256,256]{2,3,1,0:T(8,128)S(1)} fusion(f32[1,256,1024]{2,1,0:T(8,128)S(1)} %copy-done.6, s32[256]{0:T(256)S(1)} %iota_add_fusion), kind=kOutput, calls=%fused_computation.32 | convolution fusion | flops 808976384 | bytes 1311744 | tf_op jit(solution)/shard_map/dot_general | solution.py:47
  53.1 2.1 tile.45
  55.1 3.7 all-to-all-start
  59.3 25.2 %all-to-all-done = f32[2,1,1024,256]{3,0,1,2:T(2,128)S(1)} async-done(((f32[2,1,1024,256]{3,0,1,2:T(2,128)}), f32[2,1,1024,256]{3,0,1,2:T(2,128)S(1)}, u32[]{:S(2)}, u32[]{:S(2)}) %all-to-all-start) | async-done | bytes 2097184 | tf_op jit(solution)/shard_map/all_to_all | solution.py:15
  84.5 1.6 fusion.230
  86.1 5.6 %fusion.40 = f32[256,256]{1,0:T(8,128)S(1)} fusion(f32[1,1,1024,256]{3,0,1,2:T(1,128)S(1)} %get-tuple-element.12, s32[256]{0:T(256)S(1)} %iota_add_fusion.1), kind=kOutput, calls=%fused_computation.64 | convolution fusion | flops 808976384 | bytes 1311744 | tf_op jit(solution)/shard_map/kh,phw->pkw/dot_general | solution.py:63
  91.8 6.0 %fusion.42 = f32[256,256]{1,0:T(8,128)S(1)} fusion(f32[1,1,1024,256]{3,0,1,2:T(1,128)S(1)} %get-tuple-element.12, s32[256]{0:T(256)S(1)} %iota_add_fusion.1), kind=kOutput, calls=%fused_computation.66 | convolution fusion | flops 808976384 | bytes 1311744 | tf_op jit(solution)/shard_map/kh,phw->pkw/dot_general | solution.py:58
  97.8 5.6 %fusion.11 = f32[1,256,256]{1,2,0:T(8,128)S(1)} fusion(f32[256,256]{1,0:T(8,128)S(1)} %fusion.40, f32[1,1,1024,256]{3,0,1,2:T(1,128)S(1)} %get-tuple-element.11, s32[256]{0:T(256)S(1)} %iota_add_fusion.1), kind=kOutput, calls=%fused_computation.28 | convolution fusion | flops 809041920 | bytes 1573888 | tf_op jit(solution)/shard_map/kh,phw->pkw/dot_general | solution.py:58
  103.4 5.8 %fusion.121 = (f32[1,1,256,256]{2,3,1,0:T(8,128)S(1)}, f32[1,1,256,256]{2,3,1,0:T(8,128)S(1)}) fusion(f32[1,256,256]{1,2,0:T(8,128)S(1)} %fusion.11, f32[1,1,256,256]{2,3,1,0:T(8,128)S(1)} %copy.27, f32[1,1,256,256]{2,3,1,0:T(8,128)S(1)} %copy.26, f32[256,256]{1,0:T(8,128)S(1)} %fusion.42, s32[256]{0:T(256)S(1)} %iota_add_fusion.1, ...), kind=kOutput, calls=%fused_computation.143 | convolution fusion | flops 809435136 | bytes 2622464 | tf_op jit(solution)/shard_map/kh,phw->pkw/dot_general | solution.py:63
  110.2 27.2 %all-reduce.2.cloned.1.call-done = f32[2,256,256]{1,2,0:T(8,128)} async-done(((f32[2,256,256]{1,2,0:T(8,128)}), f32[2,256,256]{1,2,0:T(8,128)}) %all-reduce.2.cloned.1.call-update) | async-done | bytes 524304 | tf_op jit(solution)/shard_map/psum | solution.py:127
  137.4 1.3 copy.15
  139.2 28.2 %all_to_all.20 = f32[2,1,1024,256]{3,0,1,2:T(2,128)S(1)} all-to-all(f32[2,1,1024,256]{3,0,1,2:T(2,128)S(1)} %bitcast.183), channel_id=1, replica_groups=mesh['depth'=2,'row'=4,'col'=4] {'row'}, dimensions={2} | all-to-all | bytes 4194304 | tf_op jit(solution)/shard_map/all_to_all | solution.py:15
  167.4 1.6 fusion.229
  169.0 5.6 %fusion.36 = f32[256,256]{1,0:T(8,128)S(1)} fusion(f32[1,1,1024,256]{3,0,1,2:T(1,128)S(1)} %get-tuple-element.10, s32[256]{0:T(256)S(1)} %iota_add_fusion.1), kind=kOutput, calls=%fused_computation.60 | convolution fusion | flops 808976384 | bytes 1311744 | tf_op jit(solution)/shard_map/kh,phw->pkw/dot_general | solution.py:58
  174.7 6.0 %fusion.34 = f32[256,256]{1,0:T(8,128)S(1)} fusion(f32[1,1,1024,256]{3,0,1,2:T(1,128)S(1)} %get-tuple-element.10, s32[256]{0:T(256)S(1)} %iota_add_fusion.1), kind=kOutput, calls=%fused_computation.58 | convolution fusion | flops 808976384 | bytes 1311744 | tf_op jit(solution)/shard_map/kh,phw->pkw/dot_general | solution.py:63
  180.7 5.6 %fusion.10 = f32[1,1,256,256]{2,3,1,0:T(8,128)S(1)} fusion(f32[256,256]{1,0:T(8,128)S(1)} %fusion.36, f32[1,1,1024,256]{3,0,1,2:T(1,128)S(1)} %get-tuple-element.9, s32[256]{0:T(256)S(1)} %iota_add_fusion.1), kind=kOutput, calls=%fused_computation.26 | convolution fusion | flops 809041920 | bytes 1573888 | tf_op jit(solution)/shard_map/kh,phw->pkw/dot_general | solution.py:63
  186.4 5.8 %fusion.9 = f32[1,1,256,256]{2,3,1,0:T(8,128)S(1)} fusion(f32[256,256]{1,0:T(8,128)S(1)} %fusion.34, f32[1,1,1024,256]{3,0,1,2:T(1,128)S(1)} %get-tuple-element.9, s32[256]{0:T(256)S(1)} %iota_add_fusion.1), kind=kOutput, calls=%fused_computation.24 | convolution fusion | flops 809041920 | bytes 1573888 | tf_op jit(solution)/shard_map/kh,phw->pkw/dot_general | solution.py:58
  192.1 0.8 maximum_multiply_fusion
  193.1 44.8 %all-gather.7.cloned.1.call-done = f32[2,1,256,1024]{2,3,1,0:T(8,128)} async-done(((f32[2,1,256,256]{2,3,1,0:T(8,128)}), f32[2,1,256,1024]{2,3,1,0:T(8,128)}) %all-gather.7.cloned.1.call-update) | async-done | bytes 2097168 | tf_op jit(solution)/shard_map/all_gather | solution.py:89
  237.9 6.9 %fusion.19 = f32[256,256]{1,0:T(8,128)S(1)} fusion(f32[2,1,256,1024]{2,3,1,0:T(8,128)} %all-gather.7.cloned.1.call-done, s32[256]{0:T(256)S(1)} %iota_add_fusion), kind=kOutput, calls=%fused_computation.43 | convolution fusion | flops 808976384 | bytes 1311744 | tf_op jit(solution)/shard_map/dot_general | solution.py:47
  244.8 6.3 %fusion.8 = f32[256,256]{1,0:T(8,128)} fusion(f32[256,256]{1,0:T(8,128)S(1)} %copy-done.8, f32[256,256]{1,0:T(8,128)S(1)} %fusion.19, f32[2,1,256,1024]{2,3,1,0:T(8,128)S(1)} %copy-done.4, s32[256]{0:T(256)S(1)} %iota_add_fusion, pred[256]{0:T(512)(128)(4,1)S(1)} %get-tuple-element.22, pred[256]{0:T(512)(128)(4,1)S(1)} %get-tuple-element.23), kind=kOutput, calls=%fused_computation.22 | convolution fusion | flops 809304064 | bytes 1837056 | tf_op jit(solution)/shard_map/dot_general | solution.py:50
  251.4 26.7 %all-gather.13.cloned.1.call-done = f32[256,1024]{1,0:T(8,128)} async-done(((f32[256,256]{1,0:T(8,128)}), f32[256,1024]{1,0:T(8,128)}) %all-gather.13.cloned.1.call-update) | async-done | bytes 1048592 | tf_op jit(solution)/shard_map/all_gather | solution.py:89
  278.0 6.1 %convolution_bitcast_fusion.1 = f32[1,1,256,256]{3,2,1,0:T(8,128)S(1)} fusion(f32[256,1024]{1,0:T(8,128)} %all-gather.13.cloned.1.call-done, s32[256]{0:T(256)S(1)} %iota_add_fusion), kind=kOutput, calls=%fused_computation.18 | convolution fusion | flops 808976384 | bytes 1311744 | tf_op jit(solution)/shard_map/dot_general | solution.py:47
  284.2 4.9 %convolution_bitcast_fusion = f32[1,1,256,256]{3,2,1,0:T(8,128)S(1)} fusion(f32[256,1024]{1,0:T(8,128)S(1)} %copy-done.7, s32[256]{0:T(256)S(1)} %iota_add_fusion), kind=kOutput, calls=%fused_computation.17 | convolution fusion | flops 808976384 | bytes 1311744 | tf_op jit(solution)/shard_map/dot_general | solution.py:50
  290.1 28.2 %all_to_all.21 = f32[2,1,1024,256]{3,0,1,2:T(2,128)S(1)} all-to-all(f32[2,1,1024,256]{3,0,1,2:T(2,128)S(1)} %bitcast.184), channel_id=1, replica_groups=mesh['depth'=2,'row'=4,'col'=4] {'row'}, dimensions={2} | all-to-all | bytes 4194304 | tf_op jit(solution)/shard_map/all_to_all | solution.py:15
  318.3 1.6 fusion.228
  319.9 5.6 %fusion.28 = f32[256,256]{1,0:T(8,128)S(1)} fusion(f32[1,1,1024,256]{3,0,1,2:T(1,128)S(1)} %get-tuple-element.8, s32[256]{0:T(256)S(1)} %iota_add_fusion.1), kind=kOutput, calls=%fused_computation.52 | convolution fusion | flops 808976384 | bytes 1311744 | tf_op jit(solution)/shard_map/kh,phw->pkw/dot_general | solution.py:63
  325.6 5.8 %fusion.30 = f32[256,256]{1,0:T(8,128)S(1)} fusion(f32[1,1,1024,256]{3,0,1,2:T(1,128)S(1)} %get-tuple-element.8, s32[256]{0:T(256)S(1)} %iota_add_fusion.1), kind=kOutput, calls=%fused_computation.54 | convolution fusion | flops 808976384 | bytes 1311744 | tf_op jit(solution)/shard_map/kh,phw->pkw/dot_general | solution.py:58
  331.3 5.6 %fusion.4 = f32[1,256,256]{1,2,0:T(8,128)S(1)} fusion(f32[256,256]{1,0:T(8,128)S(1)} %fusion.28, f32[1,1,1024,256]{3,0,1,2:T(1,128)S(1)} %get-tuple-element.7, s32[256]{0:T(256)S(1)} %iota_add_fusion.1), kind=kOutput, calls=%fused_computation.14 | convolution fusion | flops 809041920 | bytes 1573888 | tf_op jit(solution)/shard_map/kh,phw->pkw/dot_general | solution.py:58
  337.0 6.1 %fusion.125 = (f32[1,1,256,256]{2,3,1,0:T(8,128)S(1)}, f32[1,1,256,256]{2,3,1,0:T(8,128)S(1)}) fusion(f32[1,256,256]{1,2,0:T(8,128)S(1)} %fusion.4, f32[1,1,256,256]{2,3,1,0:T(8,128)S(1)} %copy.27, f32[1,1,256,256]{2,3,1,0:T(8,128)S(1)} %copy.26, f32[256,256]{1,0:T(8,128)S(1)} %fusion.30, s32[256]{0:T(256)S(1)} %iota_add_fusion.1, ...), kind=kOutput, calls=%fused_computation.147 | convolution fusion | flops 809435136 | bytes 2622464 | tf_op jit(solution)/shard_map/kh,phw->pkw/dot_general | solution.py:63
  343.9 28.1 %all_to_all.22 = f32[2,1,1024,256]{3,0,1,2:T(2,128)S(1)} all-to-all(f32[2,1,1024,256]{3,0,1,2:T(2,128)S(1)} %bitcast.185), channel_id=1, replica_groups=mesh['depth'=2,'row'=4,'col'=4] {'row'}, dimensions={2} | all-to-all | bytes 4194304 | tf_op jit(solution)/shard_map/all_to_all | solution.py:15
  372.0 1.6 fusion.227
  373.6 5.6 %fusion.24 = f32[256,256]{1,0:T(8,128)S(1)} fusion(f32[1,1,1024,256]{3,0,1,2:T(1,128)S(1)} %get-tuple-element.6, s32[256]{0:T(256)S(1)} %iota_add_fusion.1), kind=kOutput, calls=%fused_computation.48 | convolution fusion | flops 808976384 | bytes 1311744 | tf_op jit(solution)/shard_map/kh,phw->pkw/dot_general | solution.py:58
  379.2 5.8 %fusion.22 = f32[256,256]{1,0:T(8,128)S(1)} fusion(f32[1,1,1024,256]{3,0,1,2:T(1,128)S(1)} %get-tuple-element.6, s32[256]{0:T(256)S(1)} %iota_add_fusion.1), kind=kOutput, calls=%fused_computation.46 | convolution fusion | flops 808976384 | bytes 1311744 | tf_op jit(solution)/shard_map/kh,phw->pkw/dot_general | solution.py:63
  385.1 5.6 %fusion.3 = f32[1,1,256,256]{2,3,1,0:T(8,128)S(1)} fusion(f32[256,256]{1,0:T(8,128)S(1)} %fusion.24, f32[1,1,1024,256]{3,0,1,2:T(1,128)S(1)} %get-tuple-element.5, s32[256]{0:T(256)S(1)} %iota_add_fusion.1), kind=kOutput, calls=%fused_computation.12 | convolution fusion | flops 809041920 | bytes 1573888 | tf_op jit(solution)/shard_map/kh,phw->pkw/dot_general | solution.py:63
  390.7 5.8 %fusion.2 = f32[1,1,256,256]{2,3,1,0:T(8,128)S(1)} fusion(f32[256,256]{1,0:T(8,128)S(1)} %fusion.22, f32[1,1,1024,256]{3,0,1,2:T(1,128)S(1)} %get-tuple-element.5, s32[256]{0:T(256)S(1)} %iota_add_fusion.1), kind=kOutput, calls=%fused_computation.10 | convolution fusion | flops 809041920 | bytes 1573888 | tf_op jit(solution)/shard_map/kh,phw->pkw/dot_general | solution.py:58
  396.5 0.8 maximum_multiply_fusion.1
  397.4 44.3 %all-gather.9.cloned.1.call-done = f32[2,1,256,1024]{2,3,1,0:T(8,128)} async-done(((f32[2,1,256,256]{2,3,1,0:T(8,128)}), f32[2,1,256,1024]{2,3,1,0:T(8,128)}) %all-gather.9.cloned.1.call-update) | async-done | bytes 2097168 | tf_op jit(solution)/shard_map/all_gather | solution.py:89
  441.7 6.9 %fusion.18 = f32[256,256]{1,0:T(8,128)S(1)} fusion(f32[2,1,256,1024]{2,3,1,0:T(8,128)} %all-gather.9.cloned.1.call-done, s32[256]{0:T(256)S(1)} %iota_add_fusion), kind=kOutput, calls=%fused_computation.40 | convolution fusion | flops 808976384 | bytes 1311744 | tf_op jit(solution)/shard_map/dot_general | solution.py:47
  448.6 5.5 %fusion.13 = f32[1,256,256]{2,1,0:T(8,128)S(1)} fusion(f32[1,256,256]{2,1,0:T(8,128)S(1)} %copy-done.3, f32[256,256]{1,0:T(8,128)S(1)} %fusion.18, f32[2,1,256,1024]{2,3,1,0:T(8,128)S(1)} %copy-done.5, s32[256]{0:T(256)S(1)} %iota_add_fusion), kind=kOutput, calls=%fused_computation.33 | convolution fusion | flops 809172992 | bytes 1836032 | tf_op jit(solution)/shard_map/dot_general | solution.py:50
  454.1 1.4 collective-permute-start
  455.6 1.3 collective-permute-start.2
  456.9 1.3 collective-permute-start.1
  458.4 4.2 collective-permute-done.2
  462.6 1.5 collective-permute-done
  464.2 1.3 fusion.128
  (51 shorter events, 5.3 us)
Async XLA Ops:
  7.2 33.1 %all-gather.11.cloned.1.call-start = ((), (), s32[]{:S(2)}) async-start(), calls=%async_computation.7 | async-start | bytes 1310720 | tf_op jit(solution)/shard_map/all_gather | solution.py:89
  40.3 6.9 %copy-start.6 = (f32[1,256,1024]{2,1,0:T(8,128)S(1)}, f32[1,256,1024]{2,1,0:T(8,128)}, u32[]{:S(2)}) copy-start(f32[1,256,1024]{2,1,0:T(8,128)} %all-gather.11.cloned.1.call-done) | copy-start | bytes 3145732
  55.1 3.8 copy-start.2
  55.1 29.4 %all-to-all-start = ((f32[2,1,1024,256]{3,0,1,2:T(2,128)}), f32[2,1,1024,256]{3,0,1,2:T(2,128)S(1)}, u32[]{:S(2)}, u32[]{:S(2)}) async-start(f32[2,1,1024,256]{3,0,1,2:T(2,128)} %bitcast.7), calls=%async_computation | async-start | bytes 4194304 | tf_op jit(solution)/shard_map/all_to_all | solution.py:15
  58.9 78.5 %all-reduce.2.cloned.1.call-start = ((), (), s32[]{:S(2)}) async-start(), calls=%async_computation.4 | async-start | bytes 1048576 | tf_op jit(solution)/shard_map/psum | solution.py:127
  110.1 127.8 %all-gather.7.cloned.1.call-start = ((), (), s32[]{:S(2)}) async-start(), calls=%async_computation.5 | async-start | bytes 2621440 | tf_op jit(solution)/shard_map/all_gather | solution.py:89
  193.0 85.0 %all-gather.13.cloned.1.call-start = ((), (), s32[]{:S(2)}) async-start(), calls=%async_computation.8 | async-start | bytes 1310720 | tf_op jit(solution)/shard_map/all_gather | solution.py:89
  193.1 51.7 %copy-start.8 = (f32[256,256]{1,0:T(8,128)S(1)}, f32[256,256]{1,0:T(8,128)}, u32[]{:S(2)}) copy-start(f32[256,256]{1,0:T(8,128)} %param.6) | copy-start | bytes 786436
  237.9 6.9 %copy-start.4 = (f32[2,1,256,1024]{2,3,1,0:T(8,128)S(1)}, f32[2,1,256,1024]{2,3,1,0:T(8,128)}, u32[]{:S(2)}) copy-start(f32[2,1,256,1024]{2,3,1,0:T(8,128)} %all-gather.7.cloned.1.call-done) | copy-start | bytes 6291460
  251.1 190.6 %all-gather.9.cloned.1.call-start = ((), (), s32[]{:S(2)}) async-start(), calls=%async_computation.6 | async-start | bytes 2621440 | tf_op jit(solution)/shard_map/all_gather | solution.py:89
  278.0 6.2 %copy-start.7 = (f32[256,1024]{1,0:T(8,128)S(1)}, f32[256,1024]{1,0:T(8,128)}, u32[]{:S(2)}) copy-start(f32[256,1024]{1,0:T(8,128)} %all-gather.13.cloned.1.call-done) | copy-start | bytes 3145732
  397.4 51.2 %copy-start.3 = (f32[1,256,256]{2,1,0:T(8,128)S(1)}, f32[1,256,256]{2,1,0:T(8,128)}, u32[]{:S(2)}) copy-start(f32[1,256,256]{2,1,0:T(8,128)} %param.4) | copy-start | bytes 786436
  441.7 6.9 %copy-start.5 = (f32[2,1,256,1024]{2,3,1,0:T(8,128)S(1)}, f32[2,1,256,1024]{2,3,1,0:T(8,128)}, u32[]{:S(2)}) copy-start(f32[2,1,256,1024]{2,3,1,0:T(8,128)} %all-gather.9.cloned.1.call-done) | copy-start | bytes 6291460
  454.1 11.4 %copy-start = (f32[1,256,256]{2,1,0:T(8,128)}, f32[1,256,256]{2,1,0:T(8,128)S(1)}, u32[]{:S(2)}) copy-start(f32[1,256,256]{2,1,0:T(8,128)S(1)} %fusion.13) | copy-start | bytes 786436
  454.1 10.1 %copy-start.1 = (f32[3,1,256,256]{3,2,1,0:T(8,128)S(1)}, f32[3,1,256,256]{3,2,1,0:T(8,128)}, u32[]{:S(2)}) copy-start(f32[3,1,256,256]{3,2,1,0:T(8,128)} %param.7) | copy-start | bytes 2359300
  454.1 9.9 %collective-permute-start = (f32[1,256,256]{2,1,0:T(8,128)S(1)}, f32[1,256,256]{2,1,0:T(8,128)S(1)}, u32[]{:S(2)}, u32[]{:S(2)}) collective-permute-start(f32[1,256,256]{2,1,0:T(8,128)S(1)} %fusion.13), channel_id=1, source_target_pairs={{16,0},{17,1},{18,2},{19,3},{20,4},{21,5},{22,6},{23,7},{24,8},{25... | collective-permute-start | bytes 786440 | tf_op jit(solution)/shard_map/ppermute | solution.py:23
  455.6 7.0 %collective-permute-start.2 = (f32[1,256,1]{2,1,0:T(8,128)S(1)}, f32[1,256,1]{2,1,0:T(8,128)S(1)}, u32[]{:S(2)}, u32[]{:S(2)}) collective-permute-start(f32[1,256,1]{2,1,0:T(8,128)S(1)} %slice.95), channel_id=1, source_target_pairs={{1,0},{2,1},{3,2},{5,4},{6,5},{7,6},{9,8},{10,9},{11,10},{13,12},{... | collective-permute-start | bytes 3080 | tf_op jit(solution)/shard_map/ppermute | solution.py:23
  456.9 5.7 %collective-permute-start.1 = (f32[1,1,256]{2,1,0:T(1,128)S(1)}, f32[1,1,256]{2,1,0:T(1,128)S(1)}, u32[]{:S(2)}, u32[]{:S(2)}) collective-permute-start(f32[1,1,256]{2,1,0:T(1,128)S(1)} %slice.93), channel_id=1, source_target_pairs={{4,0},{8,4},{12,8},{5,1},{9,5},{13,9},{6,2},{10,6},{14,10},{7,3},{... | collective-permute-start | bytes 3080 | tf_op jit(solution)/shard_map/ppermute | solution.py:23
Sparse Core Ops, SparseCore 0:
  9.5 30.6 all-gather.10
  110.2 27.1 all-reduce.1
  193.1 44.7 all-gather.6
  251.2 26.7 all-gather.12
  397.5 44.1 all-gather.8
